TPU v7x, 128 devices: a whole 4x4x4 slice. The times are simulated.
128 devices in a mesh: req: 4 (over z), exp: 32 (over x, y, core).
Axes of the slice: x: 4, y: 4, z: 4, core: 2. Of those that a mesh axis runs over, the one named last changes fastest.
Arguments:
- attn_out: bfloat16 [16384, 2048], P(('req', 'exp')), may hold values from -6 to 6
- residual: bfloat16 [16384, 2048], P(('req', 'exp')), may hold values from -6 to 6
- out_weight: bfloat16 [2048, 2048], P('exp'), may hold values from -0.125 to 0.125
- norm_gain: float32 [2048], replicated, may hold values from 0.25 to 1.75
- expert_ids: int32 [16384, 6], P(('req', 'exp')), may hold values from 0 to 31, all different within a row; in each aligned block of 128 rows (0 to 127, 128 to 255, ...) at most 36 rows name the same one
- gate_weights: float32 [16384, 6], P(('req', 'exp')), may hold values from 0.05 to 0.5
- expert_gate: bfloat16 [32, 2048, 1408], P('exp'), may hold values from -0.125 to 0.125
- expert_up: bfloat16 [32, 2048, 1408], P('exp'), may hold values from -0.125 to 0.125
- expert_down: bfloat16 [32, 1408, 2048], P('exp'), may hold values from -0.15625 to 0.15625
- shared_gate: bfloat16 [2048, 1408], P(None, 'req'), may hold values from -0.125 to 0.125
- shared_up: bfloat16 [2048, 1408], P(None, 'req'), may hold values from -0.125 to 0.125
- shared_down: bfloat16 [2048, 1408], P(None, 'req'), may hold values from -0.15625 to 0.15625
Outputs:
- mixed: bfloat16 [16384, 2048], P(('req', 'exp'))
Inputs may be any that keep to these rules, and one draw needn't show every extreme that they name: `expert_ids`: within the rows of one device no expert is named by more than 36 rows, and each row names 6 different experts.
All inputs are finite; a program needn't handle non-finite values.
Results may differ from a plain program's by a relative error of at most 0.012.
Values may be sent and summed in bfloat16 or wider, within the bound.
A program may use at most 192 MiB of HBM per device.

v0:
```python
import jax
import jax.numpy as jnp
from jax import lax
from jax.sharding import PartitionSpec as P


def body(
    attn_out,
    residual,
    out_weight,
    norm_gain,
    expert_ids,
    gate_weights,
    expert_gate,
    expert_up,
    expert_down,
    shared_gate,
    shared_up,
    shared_down,
):
    row_count, width = attn_out.shape
    topk = expert_ids.shape[1]
    experts = lax.axis_size("exp")
    capacity = min(row_count, 3 * row_count * topk // (2 * experts))
    req = lax.axis_size("req")
    quarter = out_weight.shape[0] // req
    piece = lax.dynamic_slice_in_dim(out_weight, lax.axis_index("req") * quarter, quarter, 0)
    proj = jnp.dot(
        attn_out,
        lax.all_gather(piece, ("exp", "req"), axis=0, tiled=True),
        preferred_element_type=jnp.float32,
    )
    stream = (residual.astype(jnp.float32) + proj).astype(jnp.bfloat16)
    stream_f = stream.astype(jnp.float32)
    scale = lax.rsqrt(jnp.mean(stream_f * stream_f, axis=1, keepdims=True) + 1e-06)
    normed = (stream_f * scale * norm_gain).astype(jnp.bfloat16)
    flat_ids = expert_ids.reshape(-1)
    onehot = (flat_ids[:, None] == jnp.arange(experts, dtype=jnp.int32)[None, :]).astype(jnp.int32)
    position = jnp.sum(jnp.cumsum(onehot, axis=0) * onehot, axis=1) - 1
    slot = flat_ids * capacity + position
    source_row = jnp.arange(row_count * topk, dtype=jnp.int32) // topk
    table = jnp.full((experts * capacity,), row_count, jnp.int32).at[slot].set(source_row)
    rows = jnp.arange(row_count, dtype=jnp.int32)
    pick = (table.reshape(experts, capacity)[:, :, None] == rows[None, None, :]).astype(
        jnp.bfloat16
    )
    outgoing = jnp.einsum("ecr,rd->ecd", pick, normed, preferred_element_type=jnp.float32).astype(
        jnp.bfloat16
    )
    joined = lax.all_to_all(outgoing, "exp", split_axis=0, concat_axis=0, tiled=True)
    gate_part = jnp.einsum(
        "scd,df->scf", joined, expert_gate[0], preferred_element_type=jnp.float32
    )
    up_part = jnp.einsum("scd,df->scf", joined, expert_up[0], preferred_element_type=jnp.float32)
    hidden = (jax.nn.silu(gate_part) * up_part).astype(jnp.bfloat16)
    hidden = lax.optimization_barrier(hidden)
    result = jnp.einsum(
        "scf,fd->scd", hidden, expert_down[0], preferred_element_type=jnp.float32
    ).astype(jnp.bfloat16)
    returned = lax.all_to_all(result, "exp", split_axis=0, concat_axis=0, tiled=True)
    slot_weight = (
        jnp.zeros((experts * capacity,), jnp.float32).at[slot].set(gate_weights.reshape(-1))
    )
    combine = jnp.where(
        table.reshape(experts, capacity)[None, :, :] == rows[:, None, None],
        slot_weight.reshape(experts, capacity)[None, :, :],
        0.0,
    )
    routed = jnp.einsum(
        "rec,ecd->rd",
        combine,
        returned.astype(jnp.float32),
        precision=lax.Precision.HIGHEST,
        preferred_element_type=jnp.float32,
    )
    group_rows = lax.all_gather(normed, "req", axis=0, tiled=True)
    s_gate = jnp.dot(group_rows, shared_gate, preferred_element_type=jnp.float32)
    s_up = jnp.dot(group_rows, shared_up, preferred_element_type=jnp.float32)
    s_hidden = (jax.nn.silu(s_gate) * s_up).astype(jnp.bfloat16)
    s_partial = lax.dot_general(
        s_hidden, shared_down, (((1,), (1,)), ((), ())), preferred_element_type=jnp.float32
    )
    shared = lax.psum_scatter(s_partial, "req", scatter_dimension=0, tiled=True)
    return (stream_f + routed + shared).astype(jnp.bfloat16)


def solution(mesh):
    return jax.shard_map(
        body,
        mesh=mesh,
        in_specs=(
            P(("req", "exp"), None),
            P(("req", "exp"), None),
            P("exp", None),
            P(),
            P(("req", "exp"), None),
            P(("req", "exp"), None),
            P("exp", None, None),
            P("exp", None, None),
            P("exp", None, None),
            P(None, "req"),
            P(None, "req"),
            P(None, "req"),
        ),
        out_specs=P(("req", "exp"), None),
        check_vma=False,
    )
```

profile of v0, /device:TPU:8, one launch (start us, length us, event | category | flops | bytes accessed | tf_op | source)
XLA Modules:
  0.0 291.9 jit_solution(8442988998689780267)
XLA Ops:
  6.5 0.0 copy-start
  6.5 0.0 all-gather.3.cloned.1.call-start
  6.5 1.6 constant_dynamic-slice_fusion
  8.1 0.0 all-gather.3.cloned.1.call-update
  8.1 0.8 copy.20
  8.9 0.1 eq.57
  9.1 0.1 eq.53
  9.2 1.4 copy.18
  10.6 1.7 reduce-window.6
  12.3 0.3 slice_reduce_fusion
  12.6 0.7 broadcast_multiply_fusion
  13.3 0.1 copy.19
  13.4 0.1 mul.58
  13.6 0.1 fusion.29
  13.8 3.4 %scatter_custom_fusion = s32[1152]{0:T(1024)S(1)} fusion(s32[768]{0:T(1024)S(1)} %fusion.38, s32[768]{0:T(1024)S(1)} %add_select_fusion, s32[]{:T(128)} %constant.21.clone.1), kind=kCustom, calls=%fused_computation.54 | custom fusion | bytes 4612 | tf_op jit(solution)/shard_map/scatter | solution.py:42
  17.1 0.1 eq.61
  17.2 0.0 copy-start.3
  17.3 64.5 %all-gather.3.cloned.1.call-done = bf16[2048,2048]{1,0:T(8,128)(2,1)} async-done(((bf16[16,2048]{1,0:T(8,128)(2,1)}), bf16[2048,2048]{1,0:T(8,128)(2,1)}) %all-gather.3.cloned.1.call-update) | async-done | bytes 8388624 | tf_op jit(solution)/shard_map/all_gather | solution.py:30
  81.7 5.8 %multiply_reduce_fusion = (f32[128]{0:T(128)S(1)}, f32[128,2048]{0,1:T(8,128)S(1)}) fusion(bf16[2048,2048]{1,0:T(8,128)(2,1)} %all-gather.3.cloned.1.call-done, bf16[128,2048]{1,0:T(8,128)(2,1)} %param.12, bf16[128,2048]{0,1:T(8,128)(2,1)S(1)} %copy.18), kind=kOutput, calls=%fused_computation.22 | convolution fusion | flops 1075314560 | bytes 10486272 | tf_op jit(solution)/shard_map/dot_general | solution.py:28
  87.6 0.0 copy-done.3
  87.6 0.3 multiply_convert_fusion.1
  87.9 0.0 copy-start.2
  88.0 3.9 %convolution_convert_fusion = bf16[32,36,2048]{2,1,0:T(8,128)(2,1)} fusion(bf16[128,2048]{0,1:T(8,128)(2,1)S(1)} %multiply_convert_fusion.1, s32[32,36]{1,0:T(8,128)S(1)} %eq.61), kind=kOutput, calls=%fused_computation.8 | convolution fusion | flops 606486528 | bytes 5247488 | tf_op jit(solution)/shard_map/ecr,rd->ecd/dot_general | solution.py:47
  91.9 0.0 copy-done.2
  91.9 6.3 %all-to-all-start = ((bf16[32,36,2048]{2,1,0:T(8,128)(2,1)}), bf16[32,36,2048]{2,1,0:T(8,128)(2,1)}, u32[]{:S(2)}, u32[]{:S(2)}) async-start(bf16[32,36,2048]{2,1,0:T(8,128)(2,1)} %convolution_convert_fusion), calls=%async_computation | async-start | bytes 10485760 | tf_op jit(solution)/shard_map/all_to_all | solution.py:50
  98.2 0.0 all-gather.5.cloned.1.call-start
  98.2 0.7 all-gather.5.cloned.1.call-update
  98.9 0.2 reduce-scatter.2.cloned.1.call-start
  99.1 36.2 %all-gather.5.cloned.1.call-done = bf16[512,2048]{0,1:T(8,128)(2,1)} async-done(((bf16[128,2048]{0,1:T(8,128)(2,1)}), bf16[512,2048]{0,1:T(8,128)(2,1)}) %all-gather.5.cloned.1.call-update) | async-done | bytes 2097168 | tf_op jit(solution)/shard_map/all_gather | solution.py:76
  135.3 2.9 %fusion.41 = f32[512,352]{0,1:T(8,128)S(1)} fusion(bf16[2048,352]{0,1:T(8,128)(2,1)} %param.21, bf16[512,2048]{0,1:T(8,128)(2,1)} %all-gather.5.cloned.1.call-done), kind=kOutput, calls=%fused_computation.64 | convolution fusion | flops 738197504 | bytes 4259840 | tf_op jit(solution)/shard_map/dot_general | solution.py:77
  138.3 0.0 copy-done
  138.3 6.2 %fusion.15 = f32[512,2048]{0,1:T(8,128)} fusion(bf16[2048,352]{0,1:T(8,128)(2,1)S(1)} %copy-done, bf16[2048,352]{0,1:T(8,128)(2,1)} %param.22, bf16[512,2048]{0,1:T(8,128)(2,1)} %all-gather.5.cloned.1.call-done, f32[512,352]{0,1:T(8,128)S(1)} %fusion.41), kind=kOutput, calls=%fused_computation.20 | convolution fusion | flops 1477476352 | bytes 9895936 | tf_op jit(solution)/shard_map/dot_general | solution.py:80
  144.5 0.0 reduce-scatter.2.cloned.1.call-update
  144.5 23.7 %all-to-all-done = bf16[32,36,2048]{2,1,0:T(8,128)(2,1)} async-done(((bf16[32,36,2048]{2,1,0:T(8,128)(2,1)}), bf16[32,36,2048]{2,1,0:T(8,128)(2,1)}, u32[]{:S(2)}, u32[]{:S(2)}) %all-to-all-start) | async-done | bytes 4718624 | tf_op jit(solution)/shard_map/all_to_all | solution.py:50
  168.3 0.0 slice-start
  168.3 12.2 %fusion.2 = f32[32,36,1408]{2,1,0:T(8,128)S(1)} fusion(bf16[32,36,2048]{2,1,0:T(8,128)(2,1)} %all-to-all-done, bf16[1,2048,1408]{2,1,0:T(8,128)(2,1)} %param.19), kind=kOutput, calls=%fused_computation.5 | convolution fusion | flops 6643777536 | bytes 16973824 | tf_op jit(solution)/shard_map/scd,df->scf/dot_general | solution.py:54
  180.4 0.0 slice-start.1
  180.4 12.8 %multiply_convert_fusion = bf16[32,36,1408]{2,1,0:T(8,128)(2,1)S(1)} fusion(f32[32,36,1408]{2,1,0:T(8,128)S(1)} %fusion.2, bf16[32,36,2048]{2,1,0:T(8,128)(2,1)} %all-to-all-done, bf16[1,2048,1408]{2,1,0:T(8,128)(2,1)} %param.18), kind=kOutput, calls=%fused_computation.2 | convolution fusion | flops 6653509632 | bytes 20217856 | tf_op jit(solution)/shard_map/scd,df->scf/dot_general | solution.py:51
  193.3 0.0 slice-done
  193.3 0.0 slice-done.1
  193.3 10.2 %fusion.5 = bf16[32,36,2048]{2,1,0:T(8,128)(2,1)} fusion(bf16[32,36,1408]{2,1,0:T(8,128)(2,1)S(1)} %multiply_convert_fusion, bf16[1,1408,2048]{2,1,0:T(8,128)(2,1)S(1)} %bitcast.62), kind=kOutput, calls=%fused_computation.9 | convolution fusion | flops 6646136832 | bytes 13729792 | tf_op jit(solution)/shard_map/scf,fd->scd/dot_general | solution.py:57
  203.5 0.0 copy-start.4
  203.5 5.0 %all-to-all-start.1 = ((bf16[32,36,2048]{2,1,0:T(8,128)(2,1)}), bf16[32,36,2048]{2,1,0:T(8,128)(2,1)}, u32[]{:S(2)}, u32[]{:S(2)}) async-start(bf16[32,36,2048]{2,1,0:T(8,128)(2,1)} %fusion.5), calls=%async_computation.1 | async-start | bytes 10485760 | tf_op jit(solution)/shard_map/all_to_all | solution.py:60
  208.5 0.0 copy-done.4
  208.6 0.0 copy-start.1
  208.6 0.1 copy.23
  208.7 0.1 reshape.80
  208.8 3.4 %scatter_custom_fusion.1 = f32[1152]{0:T(1024)S(1)} fusion(s32[768]{0:T(1024)S(1)} %fusion.38, f32[768]{0:T(1024)S(1)} %reshape.80, f32[]{:T(128)} %constant.44.clone.1), kind=kCustom, calls=%fused_computation.52 | custom fusion | bytes 4612 | tf_op jit(solution)/shard_map/scatter | solution.py:62
  212.2 0.1 broadcast_in_dim.29
  212.3 63.3 %all-to-all-done.1 = bf16[32,36,2048]{2,1,0:T(8,128)(2,1)} async-done(((bf16[32,36,2048]{2,1,0:T(8,128)(2,1)}), bf16[32,36,2048]{2,1,0:T(8,128)(2,1)}, u32[]{:S(2)}, u32[]{:S(2)}) %all-to-all-start.1) | async-done | bytes 4718624 | tf_op jit(solution)/shard_map/all_to_all | solution.py:60
  275.6 0.0 reduce-scatter.2.cloned.1.call-done
  275.6 8.7 %fusion.11 = bf16[128,2048]{0,1:T(8,128)(2,1)S(1)} fusion(f32[128,2048]{0,1:T(8,128)} %reduce-scatter.2.cloned.1.call-done, f32[128,2048]{0,1:T(8,128)S(1)} %get-tuple-element.6, bf16[32,36,2048]{2,1,0:T(8,128)(2,1)} %all-to-all-done.1, f32[32,36]{1,0:T(8,128)S(1)} %broadcast_in_dim.29, s32[32,36]{1,0:T(8,128)S(1)} %eq.61), kind=kOutput, calls=%fused_computation.15 | convolution fusion | flops 3624960000 | bytes 7349248 | tf_op jit(solution)/shard_map/rec,ecd->rd/dot_general | solution.py:69
  284.4 1.0 copy.27
  285.4 0.0 copy-done.1
  (7 shorter events, 0.1 us)
Async XLA Ops:
  6.5 131.7 %copy-start = (bf16[2048,352]{0,1:T(8,128)(2,1)S(1)}, bf16[2048,352]{0,1:T(8,128)(2,1)}, u32[]{:S(2)}) copy-start(bf16[2048,352]{0,1:T(8,128)(2,1)} %param.23) | copy-start | bytes 4325380
  6.5 75.2 %all-gather.3.cloned.1.call-start = ((), (), s32[]{:S(2)}) async-start(), calls=%async_computation.3 | async-start | bytes 8454144 | tf_op jit(solution)/shard_map/all_gather | solution.py:30
  17.2 70.3 %copy-start.3 = (f32[2048]{0:T(1024)S(1)}, f32[2048]{0:T(1024)}, u32[]{:S(2)}) copy-start(f32[2048]{0:T(1024)} %param.15) | copy-start | bytes 24580
  87.9 3.9 %copy-start.2 = (bf16[128,2048]{0,1:T(8,128)(2,1)}, bf16[128,2048]{0,1:T(8,128)(2,1)S(1)}, u32[]{:S(2)}) copy-start(bf16[128,2048]{0,1:T(8,128)(2,1)S(1)} %multiply_convert_fusion.1) | copy-start | bytes 1572868
  91.9 76.4 %all-to-all-start = ((bf16[32,36,2048]{2,1,0:T(8,128)(2,1)}), bf16[32,36,2048]{2,1,0:T(8,128)(2,1)}, u32[]{:S(2)}, u32[]{:S(2)}) async-start(bf16[32,36,2048]{2,1,0:T(8,128)(2,1)} %convolution_convert_fusion), calls=%async_computation | async-start | bytes 10485760 | tf_op jit(solution)/shard_map/all_to_all | solution.py:50
  98.2 37.2 %all-gather.5.cloned.1.call-start = ((), (), s32[]{:S(2)}) async-start(), calls=%async_computation.4 | async-start | bytes 2621440 | tf_op jit(solution)/shard_map/all_gather | solution.py:76
  98.9 176.7 %reduce-scatter.2.cloned.1.call-start = ((), (), s32[]{:S(2)}) async-start(), calls=%async_computation.5 | async-start | bytes 5242880 | tf_op jit(solution)/shard_map/reduce_scatter | solution.py:83
  168.3 25.0 %slice-start = ((s8[5767168]{0:T(1024)(128)(4,1)}), s8[4194304]{0:T(1024)(128)(4,1)S(1)}, s32[]{:S(2)}) async-start(s8[5767168]{0:T(1024)(128)(4,1)} %bitcast.61), calls=%async_computation.6 | async-start | bytes 8388608
  180.4 12.9 %slice-start.1 = ((s8[5767168]{0:T(1024)(128)(4,1)}), s8[1572864]{0:T(1024)(128)(4,1)S(1)}, s32[]{:S(2)}) async-start(s8[5767168]{0:T(1024)(128)(4,1)} %bitcast.61), calls=%async_computation.7 | async-start | bytes 3145728
  203.5 5.0 %copy-start.4 = (f32[128,6]{0,1:T(8,128)S(1)}, f32[128,6]{0,1:T(8,128)}, u32[]{:S(2)}) copy-start(f32[128,6]{0,1:T(8,128)} %param.17) | copy-start | bytes 9220
  203.5 72.1 %all-to-all-start.1 = ((bf16[32,36,2048]{2,1,0:T(8,128)(2,1)}), bf16[32,36,2048]{2,1,0:T(8,128)(2,1)}, u32[]{:S(2)}, u32[]{:S(2)}) async-start(bf16[32,36,2048]{2,1,0:T(8,128)(2,1)} %fusion.5), calls=%async_computation.1 | async-start | bytes 10485760 | tf_op jit(solution)/shard_map/all_to_all | solution.py:60
  208.6 76.8 %copy-start.1 = (bf16[2048,352]{0,1:T(8,128)(2,1)S(1)}, bf16[2048,352]{0,1:T(8,128)(2,1)}, u32[]{:S(2)}) copy-start(bf16[2048,352]{0,1:T(8,128)(2,1)} %param.23) | copy-start | bytes 4325380
Sparse Core Ops, SparseCore 0:
  10.5 71.1 all-gather.2
  100.7 34.6 all-gather.4
  144.7 47.8 reduce-scatter.1
where the time goes:
time: 292 us
  waiting for transfers between devices  188 us (64%)
  matrix products  62.9 us (22%)
  between operations  13.3 us (5%)
  local copies, waits for them, and re-layouts  12.8 us (4%)
  starting transfers between devices  11.5 us (4%)
  other arithmetic  2.96 us (1%)
    all_gather x1, waiting for transfers between devices, body(): lax.all_gather(piece, ('exp', 'req'), axis=0, tiled=True)  64.5 us
    all_to_all x1, waiting for transfers between devices, body(): lax.all_to_all(result, 'exp', split_axis=0, concat_axis=0, tiled=True)  63.3 us
    all_gather x1, waiting for transfers between devices, body(): group_rows = lax.all_gather(normed, 'req', axis=0, tiled=True)  36.2 us
    all_to_all x1, waiting for transfers between devices, body(): lax.all_to_all(outgoing, 'exp', split_axis=0, concat_axis=0, tiled=True)  23.7 us
    dot_general x1, matrix products, body(): jnp.einsum('scd,df->scf', joined, expert_gate[0], preferred_element_type=...  12.8 us
    dot_general x1, matrix products, body(): jnp.einsum('scd,df->scf', joined, expert_up[0], preferred_element_type=jn...  12.2 us
    dot_general x1, matrix products, body(): jnp.einsum('scf,fd->scd', hidden, expert_down[0], preferred_element_type=...  10.2 us
    dot_general x1, matrix products, body(): jnp.einsum('rec,ecd->rd', combine, returned.astype(jnp.float32), precisio...  8.73 us
  transfers between devices with their start and end apart: 5, of which 4 were waited for; matrix products, arithmetic and copies ran while one was open for 20% of the time, Pallas kernels for 0%

commit v1 on v0

--- a/solution.py
+++ b/solution.py
@@ -73,7 +73,9 @@
         precision=lax.Precision.HIGHEST,
         preferred_element_type=jnp.float32,
     )
-    group_rows = lax.all_gather(normed, "req", axis=0, tiled=True)
+    group_rows = jnp.concatenate(
+        lax.all_to_all(jnp.stack([normed] * lax.axis_size("req")), "req", 0, 0), axis=0
+    )
     s_gate = jnp.dot(group_rows, shared_gate, preferred_element_type=jnp.float32)
     s_up = jnp.dot(group_rows, shared_up, preferred_element_type=jnp.float32)
     s_hidden = (jax.nn.silu(s_gate) * s_up).astype(jnp.bfloat16)

time: 292 us -> 323 us (1.11)
  waiting for transfers between devices: 188 us -> 213 us
  starting transfers between devices: 11.5 us -> 16 us
    all_gather x1 -> x0, waiting for transfers between devices: 36.2 us -> none  [body(): group_rows = lax.all_gather(normed, 'req', axis=0, tiled=True)]
    all_to_all x1, waiting for transfers between devices: 23.7 us -> 59.6 us  [body(): lax.all_to_all(outgoing, 'exp', split_axis=0, concat_axis=0, tiled=True)]
    all_to_all x0 -> x1, waiting for transfers between devices: none -> 16.8 us  [body(): lax.all_to_all(jnp.stack([normed] * lax.axis_size('req')), 'req', 0, 0)]
    all_gather x1, waiting for transfers between devices: 64.5 us -> 72.2 us  [body(): lax.all_gather(piece, ('exp', 'req'), axis=0, tiled=True)]
    all_to_all x0 -> x1, starting transfers between devices: none -> 4.47 us  [body(): lax.all_to_all(jnp.stack([normed] * lax.axis_size('req')), 'req', 0, 0)]
  transfers between devices with their start and end apart: 5 -> 5, of which waited for: 4 -> 4; matrix products, arithmetic and copies ran while one was open for 20% -> 19% of each run, Pallas kernels for 0% -> 0%
where the time goes in v1:
time: 323 us
  waiting for transfers between devices  213 us (66%)
  matrix products  63.8 us (20%)
  starting transfers between devices  16 us (5%)
  local copies, waits for them, and re-layouts  13.9 us (4%)
  between operations  13.6 us (4%)
    all_gather x1, waiting for transfers between devices, body(): lax.all_gather(piece, ('exp', 'req'), axis=0, tiled=True)  72.2 us
    all_to_all x1, waiting for transfers between devices, body(): lax.all_to_all(result, 'exp', split_axis=0, concat_axis=0, tiled=True)  64.5 us
    all_to_all x1, waiting for transfers between devices, body(): lax.all_to_all(outgoing, 'exp', split_axis=0, concat_axis=0, tiled=True)  59.6 us
    all_to_all x1, waiting for transfers between devices, body(): lax.all_to_all(jnp.stack([normed] * lax.axis_size('req')), 'req', 0, 0)  16.8 us
    dot_general x1, matrix products, body(): jnp.einsum('scd,df->scf', joined, expert_gate[0], preferred_element_type=...  12.8 us
    dot_general x1, matrix products, body(): jnp.einsum('scd,df->scf', joined, expert_up[0], preferred_element_type=jn...  12.1 us
    dot_general x1, matrix products, body(): jnp.einsum('scf,fd->scd', hidden, expert_down[0], preferred_element_type=...  10.2 us
    dot_general x1, matrix products, body(): jnp.einsum('rec,ecd->rd', combine, returned.astype(jnp.float32), precisio...  8.73 us
  transfers between devices with their start and end apart: 5, of which 4 were waited for; matrix products, arithmetic and copies ran while one was open for 19% of the time, Pallas kernels for 0%

profile of v1, /device:TPU:8, one launch (start us, length us, event | category | flops | bytes accessed | tf_op | source)
XLA Modules:
  0.0 322.8 jit_solution(7716718514236121637)
XLA Ops:
  6.5 0.0 copy-start
  6.5 0.0 all-gather.2.cloned.1.call-start
  6.5 1.6 constant_dynamic-slice_fusion
  8.1 0.0 all-gather.2.cloned.1.call-update
  8.1 1.3 copy.19
  9.5 0.0 copy-start.3
  9.5 72.2 %all-gather.2.cloned.1.call-done = bf16[2048,2048]{1,0:T(8,128)(2,1)} async-done(((bf16[16,2048]{1,0:T(8,128)(2,1)}), bf16[2048,2048]{1,0:T(8,128)(2,1)}) %all-gather.2.cloned.1.call-update) | async-done | bytes 8388624 | tf_op jit(solution)/shard_map/all_gather | solution.py:30
  81.7 5.8 %multiply_reduce_fusion = (f32[128]{0:T(128)S(1)}, f32[128,2048]{0,1:T(8,128)S(1)}) fusion(bf16[2048,2048]{1,0:T(8,128)(2,1)} %all-gather.2.cloned.1.call-done, bf16[128,2048]{1,0:T(8,128)(2,1)} %param.12, bf16[128,2048]{0,1:T(8,128)(2,1)S(1)} %copy.19), kind=kOutput, calls=%fused_computation.22 | convolution fusion | flops 1075314560 | bytes 10486272 | tf_op jit(solution)/shard_map/dot_general | solution.py:28
  87.5 0.0 copy-start.2
  87.6 0.0 copy-done.3
  87.6 0.3 multiply_convert_fusion.1
  87.9 0.2 copy.27
  88.1 1.6 stack.2
  89.8 4.5 %all-to-all-start.2 = ((bf16[4,128,2048]{2,1,0:T(8,128)(2,1)}), bf16[4,128,2048]{2,1,0:T(8,128)(2,1)}, u32[]{:S(2)}, u32[]{:S(2)}) async-start(bf16[4,128,2048]{2,1,0:T(8,128)(2,1)} %stack.2), calls=%async_computation.2 | async-start | bytes 4194304 | tf_op jit(solution)/shard_map/all_to_all | solution.py:77
  94.2 0.0 copy-done.2
  94.3 0.1 copy.21
  94.4 0.1 eq.57
  94.5 0.1 eq.53
  94.7 1.7 reduce-window.6
  96.4 0.3 slice_reduce_fusion
  96.7 0.1 copy.20
  96.8 0.1 mul.58
  97.0 0.1 fusion.29
  97.1 3.4 %scatter_custom_fusion = s32[1152]{0:T(1024)S(1)} fusion(s32[768]{0:T(1024)S(1)} %fusion.38, s32[768]{0:T(1024)S(1)} %add_select_fusion, s32[]{:T(128)} %constant.21.clone.1), kind=kCustom, calls=%fused_computation.54 | custom fusion | bytes 4612 | tf_op jit(solution)/shard_map/scatter | solution.py:42
  100.5 0.1 eq.61
  100.6 3.9 %convolution_convert_fusion = bf16[32,36,2048]{2,1,0:T(8,128)(2,1)} fusion(bf16[128,2048]{0,1:T(8,128)(2,1)S(1)} %multiply_convert_fusion.1, s32[32,36]{1,0:T(8,128)S(1)} %eq.61), kind=kOutput, calls=%fused_computation.8 | convolution fusion | flops 606486528 | bytes 5247488 | tf_op jit(solution)/shard_map/ecr,rd->ecd/dot_general | solution.py:47
  104.5 16.8 %all-to-all-done.2 = bf16[4,128,2048]{2,1,0:T(8,128)(2,1)} async-done(((bf16[4,128,2048]{2,1,0:T(8,128)(2,1)}), bf16[4,128,2048]{2,1,0:T(8,128)(2,1)}, u32[]{:S(2)}, u32[]{:S(2)}) %all-to-all-start.2) | async-done | bytes 2097184 | tf_op jit(solution)/shard_map/all_to_all | solution.py:77
  121.3 6.3 %all-to-all-start = ((bf16[32,36,2048]{2,1,0:T(8,128)(2,1)}), bf16[32,36,2048]{2,1,0:T(8,128)(2,1)}, u32[]{:S(2)}, u32[]{:S(2)}) async-start(bf16[32,36,2048]{2,1,0:T(8,128)(2,1)} %convolution_convert_fusion), calls=%async_computation | async-start | bytes 10485760 | tf_op jit(solution)/shard_map/all_to_all | solution.py:50
  127.6 0.2 reduce-scatter.2.cloned.1.call-start
  127.8 3.8 %fusion.41 = f32[512,352]{0,1:T(8,128)} fusion(bf16[512,2048]{1,0:T(8,128)(2,1)} %bitcast.10, bf16[2048,352]{0,1:T(8,128)(2,1)} %param.21), kind=kOutput, calls=%fused_computation.64 | convolution fusion | flops 738197504 | bytes 4259840 | tf_op jit(solution)/shard_map/dot_general | solution.py:79
  131.6 0.0 copy-done
  131.6 6.4 %fusion.15 = f32[512,2048]{0,1:T(8,128)} fusion(bf16[2048,352]{0,1:T(8,128)(2,1)S(1)} %copy-done, bf16[512,2048]{1,0:T(8,128)(2,1)} %bitcast.10, bf16[2048,352]{0,1:T(8,128)(2,1)} %param.22, f32[512,352]{0,1:T(8,128)} %fusion.41), kind=kOutput, calls=%fused_computation.20 | convolution fusion | flops 1477476352 | bytes 9895936 | tf_op jit(solution)/shard_map/dot_general | solution.py:82
  138.1 0.0 reduce-scatter.2.cloned.1.call-update
  138.1 59.6 %all-to-all-done = bf16[32,36,2048]{2,1,0:T(8,128)(2,1)} async-done(((bf16[32,36,2048]{2,1,0:T(8,128)(2,1)}), bf16[32,36,2048]{2,1,0:T(8,128)(2,1)}, u32[]{:S(2)}, u32[]{:S(2)}) %all-to-all-start) | async-done | bytes 4718624 | tf_op jit(solution)/shard_map/all_to_all | solution.py:50
  197.7 0.0 slice-start
  197.7 12.1 %fusion.2 = f32[32,36,1408]{2,1,0:T(8,128)S(1)} fusion(bf16[32,36,2048]{2,1,0:T(8,128)(2,1)} %all-to-all-done, bf16[1,2048,1408]{2,1,0:T(8,128)(2,1)} %param.19), kind=kOutput, calls=%fused_computation.5 | convolution fusion | flops 6643777536 | bytes 16973824 | tf_op jit(solution)/shard_map/scd,df->scf/dot_general | solution.py:54
  209.8 0.0 slice-start.1
  209.8 12.8 %multiply_convert_fusion = bf16[32,36,1408]{2,1,0:T(8,128)(2,1)S(1)} fusion(f32[32,36,1408]{2,1,0:T(8,128)S(1)} %fusion.2, bf16[32,36,2048]{2,1,0:T(8,128)(2,1)} %all-to-all-done, bf16[1,2048,1408]{2,1,0:T(8,128)(2,1)} %param.18), kind=kOutput, calls=%fused_computation.2 | convolution fusion | flops 6653509632 | bytes 20217856 | tf_op jit(solution)/shard_map/scd,df->scf/dot_general | solution.py:51
  222.6 0.0 slice-done
  222.7 0.0 slice-done.1
  222.7 10.2 %fusion.5 = bf16[32,36,2048]{2,1,0:T(8,128)(2,1)} fusion(bf16[32,36,1408]{2,1,0:T(8,128)(2,1)S(1)} %multiply_convert_fusion, bf16[1,1408,2048]{2,1,0:T(8,128)(2,1)S(1)} %bitcast.63), kind=kOutput, calls=%fused_computation.9 | convolution fusion | flops 6646136832 | bytes 13729792 | tf_op jit(solution)/shard_map/scf,fd->scd/dot_general | solution.py:57
  232.9 0.0 copy-start.4
  232.9 5.0 %all-to-all-start.1 = ((bf16[32,36,2048]{2,1,0:T(8,128)(2,1)}), bf16[32,36,2048]{2,1,0:T(8,128)(2,1)}, u32[]{:S(2)}, u32[]{:S(2)}) async-start(bf16[32,36,2048]{2,1,0:T(8,128)(2,1)} %fusion.5), calls=%async_computation.1 | async-start | bytes 10485760 | tf_op jit(solution)/shard_map/all_to_all | solution.py:60
  237.9 0.0 copy-done.4
  237.9 0.0 copy-start.1
  237.9 0.1 copy.24
  238.1 0.1 reshape.86
  238.2 3.4 %scatter_custom_fusion.1 = f32[1152]{0:T(1024)S(1)} fusion(s32[768]{0:T(1024)S(1)} %fusion.38, f32[768]{0:T(1024)S(1)} %reshape.86, f32[]{:T(128)} %constant.44.clone.1), kind=kCustom, calls=%fused_computation.52 | custom fusion | bytes 4612 | tf_op jit(solution)/shard_map/scatter | solution.py:62
  241.6 0.1 broadcast_in_dim.29
  241.7 64.5 %all-to-all-done.1 = bf16[32,36,2048]{2,1,0:T(8,128)(2,1)} async-done(((bf16[32,36,2048]{2,1,0:T(8,128)(2,1)}), bf16[32,36,2048]{2,1,0:T(8,128)(2,1)}, u32[]{:S(2)}, u32[]{:S(2)}) %all-to-all-start.1) | async-done | bytes 4718624 | tf_op jit(solution)/shard_map/all_to_all | solution.py:60
  306.2 0.0 reduce-scatter.2.cloned.1.call-done
  306.2 8.7 %fusion.11 = bf16[128,2048]{0,1:T(8,128)(2,1)S(1)} fusion(f32[128,2048]{0,1:T(8,128)} %reduce-scatter.2.cloned.1.call-done, f32[128,2048]{0,1:T(8,128)S(1)} %get-tuple-element.6, bf16[32,36,2048]{2,1,0:T(8,128)(2,1)} %all-to-all-done.1, f32[32,36]{1,0:T(8,128)S(1)} %broadcast_in_dim.29, s32[32,36]{1,0:T(8,128)S(1)} %eq.61), kind=kOutput, calls=%fused_computation.15 | convolution fusion | flops 3624960000 | bytes 7349248 | tf_op jit(solution)/shard_map/rec,ecd->rd/dot_general | solution.py:69
  315.0 1.0 copy.29
  316.0 0.0 copy-done.1
  (8 shorter events, 0.1 us)
Async XLA Ops:
  6.5 125.1 %copy-start = (bf16[2048,352]{0,1:T(8,128)(2,1)S(1)}, bf16[2048,352]{0,1:T(8,128)(2,1)}, u32[]{:S(2)}) copy-start(bf16[2048,352]{0,1:T(8,128)(2,1)} %param.23) | copy-start | bytes 4325380
  6.5 75.2 %all-gather.2.cloned.1.call-start = ((), (), s32[]{:S(2)}) async-start(), calls=%async_computation.4 | async-start | bytes 8454144 | tf_op jit(solution)/shard_map/all_gather | solution.py:30
  9.5 78.1 %copy-start.3 = (f32[2048]{0:T(1024)S(1)}, f32[2048]{0:T(1024)}, u32[]{:S(2)}) copy-start(f32[2048]{0:T(1024)} %param.15) | copy-start | bytes 24580
  87.5 6.7 %copy-start.2 = (s32[128,6]{0,1:T(8,128)S(1)}, s32[128,6]{0,1:T(8,128)}, u32[]{:S(2)}) copy-start(s32[128,6]{0,1:T(8,128)} %param.16) | copy-start | bytes 9220
  89.8 31.5 %all-to-all-start.2 = ((bf16[4,128,2048]{2,1,0:T(8,128)(2,1)}), bf16[4,128,2048]{2,1,0:T(8,128)(2,1)}, u32[]{:S(2)}, u32[]{:S(2)}) async-start(bf16[4,128,2048]{2,1,0:T(8,128)(2,1)} %stack.2), calls=%async_computation.2 | async-start | bytes 4194304 | tf_op jit(solution)/shard_map/all_to_all | solution.py:77
  121.3 76.4 %all-to-all-start = ((bf16[32,36,2048]{2,1,0:T(8,128)(2,1)}), bf16[32,36,2048]{2,1,0:T(8,128)(2,1)}, u32[]{:S(2)}, u32[]{:S(2)}) async-start(bf16[32,36,2048]{2,1,0:T(8,128)(2,1)} %convolution_convert_fusion), calls=%async_computation | async-start | bytes 10485760 | tf_op jit(solution)/shard_map/all_to_all | solution.py:50
  127.6 178.6 %reduce-scatter.2.cloned.1.call-start = ((), (), s32[]{:S(2)}) async-start(), calls=%async_computation.5 | async-start | bytes 5242880 | tf_op jit(solution)/shard_map/reduce_scatter | solution.py:85
  197.7 24.9 %slice-start = ((s8[5767168]{0:T(1024)(128)(4,1)}), s8[4194304]{0:T(1024)(128)(4,1)S(1)}, s32[]{:S(2)}) async-start(s8[5767168]{0:T(1024)(128)(4,1)} %bitcast.62), calls=%async_computation.6 | async-start | bytes 8388608
  209.8 12.8 %slice-start.1 = ((s8[5767168]{0:T(1024)(128)(4,1)}), s8[1572864]{0:T(1024)(128)(4,1)S(1)}, s32[]{:S(2)}) async-start(s8[5767168]{0:T(1024)(128)(4,1)} %bitcast.62), calls=%async_computation.7 | async-start | bytes 3145728
  232.9 5.0 %copy-start.4 = (f32[128,6]{0,1:T(8,128)S(1)}, f32[128,6]{0,1:T(8,128)}, u32[]{:S(2)}) copy-start(f32[128,6]{0,1:T(8,128)} %param.17) | copy-start | bytes 9220
  232.9 73.3 %all-to-all-start.1 = ((bf16[32,36,2048]{2,1,0:T(8,128)(2,1)}), bf16[32,36,2048]{2,1,0:T(8,128)(2,1)}, u32[]{:S(2)}, u32[]{:S(2)}) async-start(bf16[32,36,2048]{2,1,0:T(8,128)(2,1)} %fusion.5), calls=%async_computation.1 | async-start | bytes 10485760 | tf_op jit(solution)/shard_map/all_to_all | solution.py:60
  237.9 78.0 %copy-start.1 = (bf16[2048,352]{0,1:T(8,128)(2,1)S(1)}, bf16[2048,352]{0,1:T(8,128)(2,1)}, u32[]{:S(2)}) copy-start(bf16[2048,352]{0,1:T(8,128)(2,1)} %param.23) | copy-start | bytes 4325380
Sparse Core Ops, SparseCore 0:
  10.5 71.1 all-gather.1
  138.2 46.4 reduce-scatter.1
